TPU v7x, 32 devices: a whole 2x2x4 slice. The times are simulated.
32 devices in a mesh: shard: 2 (over x), ctx: 4 (over y, core), tp: 4 (over z).
Axes of the slice: x: 2, y: 2, z: 4, core: 2. Of those that a mesh axis runs over, the one named last changes fastest.
Arguments:
- tokens: bfloat16 [4, 4096, 1024], P('shard', ('ctx', 'tp')), may hold values from -6 to 6
- positions: int32 [4, 4096], P('shard', 'ctx'), may hold values from 0 to 12287, as said below
- first_gain: float32 [1024], replicated, may hold values from 0.5 to 1.5
- query_weight: bfloat16 [1024, 1024], P(('shard', 'ctx'), 'tp'), may hold values from -0.1875 to 0.1875
- key_weight: bfloat16 [1024, 512], P(('shard', 'ctx'), 'tp'), may hold values from -0.1875 to 0.1875
- value_weight: bfloat16 [1024, 512], P(('shard', 'ctx'), 'tp'), may hold values from -0.1875 to 0.1875
- query_gain: float32 [64], replicated, may hold values from 0.1 to 1.9
- key_gain: float32 [64], replicated, may hold values from 0.1 to 1.9
- output_weight: bfloat16 [1024, 1024], P('tp', ('shard', 'ctx')), may hold values from -1 to 1
- second_gain: float32 [1024], replicated, may hold values from 0.5 to 1.5
- gate_weight: bfloat16 [1024, 4608], P(('shard', 'ctx'), 'tp'), may hold values from -0.1875 to 0.1875
- up_weight: bfloat16 [1024, 4608], P(('shard', 'ctx'), 'tp'), may hold values from -0.1875 to 0.1875
- down_weight: bfloat16 [4608, 1024], P('tp', ('shard', 'ctx')), may hold values from -0.09375 to 0.09375
- upstream: bfloat16 [4, 4096, 1024], P('shard', ('ctx', 'tp')), may hold values from -6 to 6
Outputs:
- block_output: bfloat16 [4, 4096, 1024], P('shard', ('ctx', 'tp'))
- token_gradient: float32 [4, 4096, 1024], P('shard', ('ctx', 'tp'))
- query_gradient: float32 [1024, 1024], P(('shard', 'ctx'), 'tp')
- key_gradient: float32 [1024, 512], P(('shard', 'ctx'), 'tp')
- value_gradient: float32 [1024, 512], P(('shard', 'ctx'), 'tp')
- output_gradient: float32 [1024, 1024], P('tp', ('shard', 'ctx'))
- gate_gradient: float32 [1024, 4608], P(('shard', 'ctx'), 'tp')
- up_gradient: float32 [1024, 4608], P(('shard', 'ctx'), 'tp')
- down_gradient: float32 [4608, 1024], P('tp', ('shard', 'ctx'))
- first_gain_gradient: float32 [1024], replicated
- second_gain_gradient: float32 [1024], replicated
- query_gain_gradient: float32 [64], replicated
- key_gain_gradient: float32 [64], replicated
Inputs may be any that keep to these rules, and one draw needn't show every extreme that they name: `positions`: along each sequence a position exceeds the one before it by 1 to 3; the first is at most 2.
All inputs are finite; a program needn't handle non-finite values.
Results may differ from a plain program's by a relative error of at most 0.02.
Values may be sent and summed in bfloat16 or wider, within the bound.
No kernel may reach another device: no remote copies, remote signals or barrier semaphores. Data moves between devices by JAX's collectives and lax.ppermute only.
A program may use at most 192 MiB of HBM per device.

v0:
```python
import math
import jax
import jax.numpy as jnp
from jax import lax
from jax.sharding import PartitionSpec as P

EPS = 1e-05
THETA = 1000000.0
NEGATIVE = -1e30


def norm_rows(values, gain):
    return values * lax.rsqrt(jnp.mean(values * values, axis=-1, keepdims=True) + EPS) * gain


def rotary_tables(places, width):
    freqs = jnp.exp(-math.log(THETA) * jnp.arange(0, width, 2).astype(jnp.float32) / width)
    angles = places.astype(jnp.float32)[:, None] * freqs[None, :]
    cosine = jnp.concatenate([jnp.cos(angles), jnp.cos(angles)], axis=-1)[:, None, :]
    sine = jnp.concatenate([jnp.sin(angles), jnp.sin(angles)], axis=-1)[:, None, :]
    return (cosine, sine)


def shape_heads(raw, gain, cosine, sine):
    normed = norm_rows(raw, gain)
    half = normed.shape[-1] // 2
    turned = jnp.concatenate([-normed[..., half:], normed[..., :half]], axis=-1)
    return normed * cosine + turned * sine


def dot_first(left, right):
    return lax.dot_general(
        left, right, (((0,), (0,)), ((), ())), preferred_element_type=jnp.float32
    )


def dot_last(left, right):
    return lax.dot_general(
        left, right, (((1,), (1,)), ((), ())), preferred_element_type=jnp.float32
    )


def project_rows(left, right):
    return jnp.dot(left, right, preferred_element_type=jnp.float32)


def project_pair(gate_back, gate_full, up_back, up_full):
    first_part = dot_last(gate_back, gate_full)
    return first_part + dot_last(up_back, up_full)


def project_three(query_back, query_full, key_back, key_full, value_back, value_full):
    total = dot_last(query_back, query_full)
    total = total + dot_last(key_back, key_full)
    return total + dot_last(value_back, value_full)


def fetch_weights(
    query_weight, key_weight, value_weight, output_weight, gate_weight, up_weight, down_weight
):
    return (
        lax.all_gather(query_weight, ("shard", "ctx"), axis=0, tiled=True),
        lax.all_gather(key_weight, ("shard", "ctx"), axis=0, tiled=True),
        lax.all_gather(value_weight, ("shard", "ctx"), axis=0, tiled=True),
        lax.all_gather(output_weight, ("shard", "ctx"), axis=1, tiled=True),
        lax.all_gather(gate_weight, ("shard", "ctx"), axis=0, tiled=True),
        lax.all_gather(up_weight, ("shard", "ctx"), axis=0, tiled=True),
        lax.all_gather(down_weight, ("shard", "ctx"), axis=1, tiled=True),
    )


def attend(query_b, key_b, value_b, first_query):
    span_rows, kv_heads, group, width = query_b.shape
    scale = 1.0 / math.sqrt(width)
    query_index = first_query + jnp.arange(span_rows)
    last_query = first_query + span_rows - 1
    init = (
        jnp.full((kv_heads, group, span_rows), NEGATIVE, jnp.float32),
        jnp.zeros((kv_heads, group, span_rows), jnp.float32),
        jnp.zeros((kv_heads, group, span_rows, width), jnp.float32),
    )
    key_piece = lax.all_gather(key_b, "ctx", axis=0, tiled=True)
    value_piece = lax.all_gather(value_b, "ctx", axis=0, tiled=True)

    def update(state):
        peak, total, accum = state
        scores = (
            jnp.einsum("qkgd,nkd->kgqn", query_b, key_piece, preferred_element_type=jnp.float32)
            * scale
        )
        key_index = jnp.arange(key_piece.shape[0])
        allowed = key_index[None, :] <= query_index[:, None]
        masked = jnp.where(allowed, scores, NEGATIVE)
        new_peak = jnp.maximum(peak, jnp.max(masked, axis=-1))
        weights = jnp.where(allowed, jnp.exp(masked - new_peak[..., None]), 0.0)
        total = jnp.sum(weights, axis=-1)
        accum = jnp.einsum(
            "kgqn,nkd->kgqd",
            weights.astype(jnp.bfloat16),
            value_piece,
            preferred_element_type=jnp.float32,
        )
        return (new_peak, total, accum)

    peak, total, accum = lax.cond(jnp.int32(0) <= last_query, update, lambda state: state, init)
    return (accum / total[..., None], peak + jnp.log(total))


def attend_back(query_b, keys_all, values_all, back_b, attention, logsum, first_query):
    span_rows, kv_heads, group, width = query_b.shape
    scale = 1.0 / math.sqrt(width)
    query_index = first_query + jnp.arange(span_rows)
    delta = jnp.einsum("qkgd,kgqd->kgq", back_b.astype(jnp.float32), attention)

    def block(index, carry):
        query_back, key_buffer, value_buffer = carry
        key_block = lax.dynamic_slice_in_dim(keys_all, index * span_rows, span_rows, 0)
        value_block = lax.dynamic_slice_in_dim(values_all, index * span_rows, span_rows, 0)
        scores = (
            jnp.einsum("qkgd,nkd->kgqn", query_b, key_block, preferred_element_type=jnp.float32)
            * scale
        )
        key_index = index * span_rows + jnp.arange(span_rows)
        allowed = key_index[None, :] <= query_index[:, None]
        probs = jnp.where(allowed, jnp.exp(scores - logsum[..., None]), 0.0)
        value_part = jnp.einsum(
            "kgqn,qkgd->nkd", probs.astype(jnp.bfloat16), back_b, preferred_element_type=jnp.float32
        )
        slopes = jnp.einsum(
            "qkgd,nkd->kgqn", back_b, value_block, preferred_element_type=jnp.float32
        )
        score_back = (probs * (slopes - delta[..., None])).astype(jnp.bfloat16)
        query_back = (
            query_back
            + jnp.einsum(
                "kgqn,nkd->qkgd", score_back, key_block, preferred_element_type=jnp.float32
            )
            * scale
        )
        key_part = (
            jnp.einsum("kgqn,qkgd->nkd", score_back, query_b, preferred_element_type=jnp.float32)
            * scale
        )
        key_buffer = lax.dynamic_update_slice_in_dim(key_buffer, key_part, index * span_rows, 0)
        value_buffer = lax.dynamic_update_slice_in_dim(
            value_buffer, value_part, index * span_rows, 0
        )
        return (query_back, key_buffer, value_buffer)

    init = (
        jnp.zeros(query_b.shape, jnp.float32),
        jnp.zeros(keys_all.shape, jnp.float32),
        jnp.zeros(values_all.shape, jnp.float32),
    )
    return lax.fori_loop(0, first_query // span_rows + 1, block, init)


def per_device(
    tokens,
    positions,
    first_gain,
    query_weight,
    key_weight,
    value_weight,
    query_gain,
    key_gain,
    output_weight,
    second_gain,
    gate_weight,
    up_weight,
    down_weight,
    upstream,
):
    sequences, rows, width = tokens.shape
    span_rows = positions.shape[1]
    head_dim = query_gain.shape[0]
    first_query = lax.axis_index("ctx") * span_rows
    query_acc = jnp.zeros((width, query_weight.shape[1]), jnp.float32)
    key_acc = jnp.zeros((width, key_weight.shape[1]), jnp.float32)
    value_acc = jnp.zeros((width, value_weight.shape[1]), jnp.float32)
    output_acc = jnp.zeros((output_weight.shape[0], width), jnp.float32)
    gate_acc = jnp.zeros((width, gate_weight.shape[1]), jnp.float32)
    up_acc = jnp.zeros((width, up_weight.shape[1]), jnp.float32)
    down_acc = jnp.zeros((down_weight.shape[0], width), jnp.float32)
    first_gain_acc = jnp.zeros_like(first_gain)
    second_gain_acc = jnp.zeros_like(second_gain)
    query_gain_acc = jnp.zeros_like(query_gain)
    key_gain_acc = jnp.zeros_like(key_gain)
    results = []
    gradients = []
    for seq in range(sequences):
        current = fetch_weights(
            query_weight,
            key_weight,
            value_weight,
            output_weight,
            gate_weight,
            up_weight,
            down_weight,
        )
        query_full, key_full, value_full, output_full, gate_full, up_full, down_full = current
        token_rows = tokens[seq].astype(jnp.float32)
        first = norm_rows(token_rows, first_gain).astype(jnp.bfloat16)
        first_all = lax.all_gather(first, "tp", axis=0, tiled=True)
        cosine, sine = rotary_tables(positions[seq], head_dim)
        query_raw = jnp.dot(first_all, query_full, preferred_element_type=jnp.float32).reshape(
            span_rows, -1, head_dim
        )
        key_raw = jnp.dot(first_all, key_full, preferred_element_type=jnp.float32).reshape(
            span_rows, -1, head_dim
        )
        value_b = (
            jnp.dot(first_all, value_full, preferred_element_type=jnp.float32)
            .astype(jnp.bfloat16)
            .reshape(span_rows, -1, head_dim)
        )
        kv_heads = key_raw.shape[1]
        group = query_raw.shape[1] // kv_heads

        def query_shape(raw, gain):
            return shape_heads(raw, gain, cosine, sine)

        query_b = (
            query_shape(query_raw, query_gain)
            .astype(jnp.bfloat16)
            .reshape(span_rows, kv_heads, group, head_dim)
        )
        key_b = query_shape(key_raw, key_gain).astype(jnp.bfloat16)
        attention, logsum = attend(query_b, key_b, value_b, first_query)
        mixed_b = jnp.transpose(attention, (2, 0, 1, 3)).reshape(span_rows, -1).astype(jnp.bfloat16)
        attn_rows = lax.psum_scatter(
            project_rows(mixed_b, output_full).astype(jnp.bfloat16),
            "tp",
            scatter_dimension=0,
            tiled=True,
        ).astype(jnp.float32)
        middle = token_rows + attn_rows
        second = norm_rows(middle, second_gain).astype(jnp.bfloat16)
        second_all = lax.all_gather(second, "tp", axis=0, tiled=True)
        gate = jnp.dot(second_all, gate_full, preferred_element_type=jnp.float32)
        up = jnp.dot(second_all, up_full, preferred_element_type=jnp.float32)
        gate_sig = jax.nn.sigmoid(gate)
        swish = gate * gate_sig
        hidden_b = (swish * up).astype(jnp.bfloat16)
        ffn_rows = lax.psum_scatter(
            project_rows(hidden_b, down_full).astype(jnp.bfloat16),
            "tp",
            scatter_dimension=0,
            tiled=True,
        ).astype(jnp.float32)
        results.append((middle + ffn_rows).astype(jnp.bfloat16))
        current = fetch_weights(
            query_weight,
            key_weight,
            value_weight,
            output_weight,
            gate_weight,
            up_weight,
            down_weight,
        )
        query_full, key_full, value_full, output_full, gate_full, up_full, down_full = current
        upstream_b = upstream[seq]
        upstream_all = lax.all_gather(upstream_b, "tp", axis=0, tiled=True)
        down_acc = down_acc + dot_first(hidden_b, upstream_all)
        hidden_back = dot_last(upstream_all, down_full)
        gate_back = (hidden_back * up * (gate_sig * (1.0 + gate * (1.0 - gate_sig)))).astype(
            jnp.bfloat16
        )
        up_back = (hidden_back * swish).astype(jnp.bfloat16)
        gate_acc = gate_acc + dot_first(second_all, gate_back)
        up_acc = up_acc + dot_first(second_all, up_back)
        second_back = lax.psum_scatter(
            project_pair(gate_back, gate_full, up_back, up_full).astype(jnp.bfloat16),
            "tp",
            scatter_dimension=0,
            tiled=True,
        ).astype(jnp.float32)
        unused_second, second_fn = jax.vjp(norm_rows, middle, second_gain)
        middle_part, second_part = second_fn(second_back)
        second_gain_acc = second_gain_acc + second_part
        middle_back = upstream_b.astype(jnp.float32) + middle_part
        mixed_back_all = lax.all_gather(middle_back.astype(jnp.bfloat16), "tp", axis=0, tiled=True)
        output_acc = output_acc + dot_first(mixed_b, mixed_back_all)
        attention_back = (
            dot_last(mixed_back_all, output_full)
            .astype(jnp.bfloat16)
            .reshape(span_rows, kv_heads, group, head_dim)
        )
        keys_all, values_all = (
            lax.all_gather(key_b, "ctx", axis=0, tiled=True),
            lax.all_gather(value_b, "ctx", axis=0, tiled=True),
        )
        query_back, key_buffer, value_buffer = attend_back(
            query_b, keys_all, values_all, attention_back, attention, logsum, first_query
        )
        key_back, value_back = (
            lax.psum_scatter(
                key_buffer.astype(jnp.bfloat16), "ctx", scatter_dimension=0, tiled=True
            ).astype(jnp.float32),
            lax.psum_scatter(
                value_buffer.astype(jnp.bfloat16), "ctx", scatter_dimension=0, tiled=True
            ).astype(jnp.float32),
        )
        value_back_b = value_back.reshape(span_rows, -1).astype(jnp.bfloat16)
        unused_key, key_fn = jax.vjp(query_shape, key_raw, key_gain)
        key_raw_back, key_gain_part = key_fn(key_back)
        unused_query, query_fn = jax.vjp(query_shape, query_raw, query_gain)
        query_raw_back, query_gain_part = query_fn(query_back.reshape(span_rows, -1, head_dim))
        key_raw_b = key_raw_back.reshape(span_rows, -1).astype(jnp.bfloat16)
        query_raw_b = query_raw_back.reshape(span_rows, -1).astype(jnp.bfloat16)
        key_gain_acc = key_gain_acc + key_gain_part
        query_gain_acc = query_gain_acc + query_gain_part
        query_acc = query_acc + dot_first(first_all, query_raw_b)
        key_acc = key_acc + dot_first(first_all, key_raw_b)
        value_acc = value_acc + dot_first(first_all, value_back_b)
        first_back = lax.psum_scatter(
            project_three(
                query_raw_b, query_full, key_raw_b, key_full, value_back_b, value_full
            ).astype(jnp.bfloat16),
            "tp",
            scatter_dimension=0,
            tiled=True,
        ).astype(jnp.float32)
        unused_first, first_fn = jax.vjp(norm_rows, token_rows, first_gain)
        token_part, first_part = first_fn(first_back)
        first_gain_acc = first_gain_acc + first_part
        gradients.append(middle_back + token_part)
    query_out, key_out, value_out, output_out, gate_out, up_out, down_out = (
        lax.psum_scatter(query_acc, ("shard", "ctx"), scatter_dimension=0, tiled=True),
        lax.psum_scatter(key_acc, ("shard", "ctx"), scatter_dimension=0, tiled=True),
        lax.psum_scatter(value_acc, ("shard", "ctx"), scatter_dimension=0, tiled=True),
        lax.psum_scatter(output_acc, ("shard", "ctx"), scatter_dimension=1, tiled=True),
        lax.psum_scatter(gate_acc, ("shard", "ctx"), scatter_dimension=0, tiled=True),
        lax.psum_scatter(up_acc, ("shard", "ctx"), scatter_dimension=0, tiled=True),
        lax.psum_scatter(down_acc, ("shard", "ctx"), scatter_dimension=1, tiled=True),
    )
    first_total, second_total, query_total, key_total = lax.psum(
        (first_gain_acc, second_gain_acc, query_gain_acc, key_gain_acc), ("shard", "ctx", "tp")
    )
    return (
        jnp.stack(results),
        jnp.stack(gradients),
        query_out,
        key_out,
        value_out,
        output_out,
        gate_out,
        up_out,
        down_out,
        first_total,
        second_total,
        query_total,
        key_total,
    )


def solution(mesh):
    in_specs = (
        P("shard", ("ctx", "tp"), None),
        P("shard", "ctx"),
        P(),
        P(("shard", "ctx"), "tp"),
        P(("shard", "ctx"), "tp"),
        P(("shard", "ctx"), "tp"),
        P(),
        P(),
        P("tp", ("shard", "ctx")),
        P(),
        P(("shard", "ctx"), "tp"),
        P(("shard", "ctx"), "tp"),
        P("tp", ("shard", "ctx")),
        P("shard", ("ctx", "tp"), None),
    )
    out_specs = (
        P("shard", ("ctx", "tp"), None),
        P("shard", ("ctx", "tp"), None),
        P(("shard", "ctx"), "tp"),
        P(("shard", "ctx"), "tp"),
        P(("shard", "ctx"), "tp"),
        P("tp", ("shard", "ctx")),
        P(("shard", "ctx"), "tp"),
        P(("shard", "ctx"), "tp"),
        P("tp", ("shard", "ctx")),
        P(),
        P(),
        P(),
        P(),
    )
    return jax.shard_map(
        per_device, mesh=mesh, in_specs=in_specs, out_specs=out_specs, check_vma=False
    )
```

profile of v0, /device:TPU:0, one launch (start us, length us, event | category | flops | bytes accessed | tf_op | source)
XLA Modules:
  0.0 1653.8 jit_solution(1743868269783206539)
XLA Ops:
  14.1 10.8 all_gather.39
  26.7 35.4 %all-gather.18.cloned.1.call-done = bf16[1024,1024]{1,0:T(8,128)(2,1)} async-done(((bf16[256,1024]{1,0:T(8,128)(2,1)}), bf16[1024,1024]{1,0:T(8,128)(2,1)}) %all-gather.18.cloned.1.call-update) | async-done | bytes 2097168 | tf_op jit(solution)/shard_map/all_gather | solution.py:204
  65.1 43.7 %all-gather.32.cloned.1.call-done = bf16[1024,1024]{1,0:T(8,128)(2,1)} async-done(((bf16[256,1024]{1,0:T(8,128)(2,1)}), bf16[1024,1024]{1,0:T(8,128)(2,1)}) %all-gather.32.cloned.1.call-update) | async-done | bytes 2097168 | tf_op jit(solution)/shard_map/all_gather | solution.py:204
  114.0 9.6 all_gather.42
  125.2 10.8 all_gather.41
  140.3 12.0 all_gather.88
  164.3 84.7 %conditional.2 = (f32[2,2,1024]{2,1,0:T(2,128)}, f32[2,2,1024]{2,1,0:T(2,128)}, f32[2,2,1024,64]{2,3,1,0:T(8,128)S(1)}, f32[2,2,1024]{2,1,0:T(2,128)S(1)}) conditional(s32[]{:T(128)} %convert_element_type.260, () %tuple.36, (s32[1024]{0:T(1024)S(1)}, bf16[4096,2,64]{0,2,1:T(8,128)(2,1)}, bf16[1024,2,2,64]{0,3,2,1:T(8,128)(2,1)}, ...), branch_computations={%region_3.0_spmd, %region_4.7_spmd} | conditional | flops 4517261312 | bytes 226103360 | solution.py:105
  170.2 27.5 %fusion.4 = (f32[2,2,1024]{2,1,0:T(2,128)S(1)}, f32[2,4096,1024,2]{2,1,3,0:T(8,128)}) fusion(pred[1024,4096]{0,1:T(8,128)(4,1)} %iota_compare_fusion, bf16[1024,2,2,64]{0,3,2,1:T(8,128)(2,1)} %get-tuple-element.116, bf16[4096,2,64]{0,2,1:T(8,128)(2,1)} %get-tuple-element.115), kind=kOutput, calls=%fused_computation.4 | convolution fusion | flops 2197811200 | bytes 72892416 | tf_op jit(solution)/shard_map/cond/branch_1_fun/qkgd,nkd->kgqn/dot_general | solution.py:88
  198.3 23.9 %fusion.6 = f32[2,2,1024]{2,1,0:T(2,128)} fusion(f32[2,4096,1024,2]{2,1,3,0:T(8,128)} %get-tuple-element.326, f32[2,2,1024]{2,1,0:T(2,128)} %broadcast_maximum_fusion, pred[1024,4096]{0,1:T(8,128)(4,1)} %iota_compare_fusion), kind=kLoop, calls=%fused_computation.6 | loop fusion | flops 83881984 | bytes 71335936 | tf_op jit(solution)/shard_map/cond/branch_1_fun/reduce_sum | solution.py:96
  222.2 26.1 %fusion.7 = f32[2,2,1024,64]{2,3,1,0:T(8,128)S(1)} fusion(f32[2,4096,1024,2]{2,1,3,0:T(8,128)} %get-tuple-element.326, f32[2,2,1024]{2,1,0:T(2,128)} %broadcast_maximum_fusion, pred[1024,4096]{0,1:T(8,128)(4,1)} %iota_compare_fusion, bf16[4096,2,64]{0,2,1:T(8,128)(2,1)S(1)} %copy-done.129), kind=kOutput, calls=%fused_computation.7 | convolution fusion | flops 2231369728 | bytes 73416704 | tf_op jit(solution)/shard_map/cond/branch_1_fun/kgqn,nkd->kgqd/dot_general | solution.py:97
  252.9 83.4 %conditional.3 = (f32[2,2,1024]{2,1,0:T(2,128)}, f32[2,2,1024]{2,1,0:T(2,128)}, f32[2,2,1024,64]{2,3,1,0:T(8,128)S(1)}, f32[2,2,1024]{2,1,0:T(2,128)S(1)}) conditional(s32[]{:T(128)} %convert_element_type.260, () %tuple.38, (s32[1024]{0:T(1024)S(1)}, bf16[4096,2,64]{0,2,1:T(8,128)(2,1)}, bf16[1024,2,2,64]{0,3,2,1:T(8,128)(2,1)S(1)}, ...), branch_computations={%region_13.14_spmd, %region_14.17_spmd} | conditional | flops 4517261312 | bytes 230297696 | solution.py:105
  258.8 25.9 %fusion.16 = (f32[2,2,1024]{2,1,0:T(2,128)S(1)}, f32[2,4096,1024,2]{2,1,3,0:T(8,128)}) fusion(pred[1024,4096]{0,1:T(8,128)(4,1)} %iota_compare_fusion.1, bf16[1024,2,2,64]{0,3,2,1:T(8,128)(2,1)S(1)} %get-tuple-element.120, bf16[4096,2,64]{0,2,1:T(8,128)(2,1)S(1)} %copy-done.37), kind=kOutput, calls=%fused_computation.19 | convolution fusion | flops 2197811200 | bytes 72892416 | tf_op jit(solution)/shard_map/cond/branch_1_fun/qkgd,nkd->kgqn/dot_general | solution.py:88
  285.4 24.1 %fusion.18 = f32[2,2,1024]{2,1,0:T(2,128)} fusion(f32[2,4096,1024,2]{2,1,3,0:T(8,128)} %get-tuple-element.328, f32[2,2,1024]{2,1,0:T(2,128)} %broadcast_maximum_fusion.1, pred[1024,4096]{0,1:T(8,128)(4,1)} %iota_compare_fusion.1), kind=kLoop, calls=%fused_computation.21 | loop fusion | flops 83881984 | bytes 71335936 | tf_op jit(solution)/shard_map/cond/branch_1_fun/reduce_sum | solution.py:96
  309.4 26.1 %fusion.19 = f32[2,2,1024,64]{2,3,1,0:T(8,128)S(1)} fusion(f32[2,4096,1024,2]{2,1,3,0:T(8,128)} %get-tuple-element.328, f32[2,2,1024]{2,1,0:T(2,128)} %broadcast_maximum_fusion.1, pred[1024,4096]{0,1:T(8,128)(4,1)} %iota_compare_fusion.1, bf16[4096,2,64]{0,2,1:T(8,128)(2,1)S(1)} %copy-done.128), kind=kOutput, calls=%fused_computation.22 | convolution fusion | flops 2231369728 | bytes 73416704 | tf_op jit(solution)/shard_map/cond/branch_1_fun/kgqn,nkd->kgqd/dot_general | solution.py:97
  340.0 42.3 %reduce-scatter.24.cloned.1.call-done = bf16[256,1024]{1,0:T(8,128)(2,1)} async-done(((bf16[1024,1024]{1,0:T(8,128)(2,1)}), bf16[256,1024]{1,0:T(8,128)(2,1)}) %reduce-scatter.24.cloned.1.call-update) | async-done | bytes 524304 | tf_op jit(solution)/shard_map/reduce_scatter | solution.py:231
  391.0 40.7 %all-gather.24.cloned.1.call-done = bf16[1024,1024]{1,0:T(8,128)(2,1)} async-done(((bf16[256,1024]{1,0:T(8,128)(2,1)}), bf16[1024,1024]{1,0:T(8,128)(2,1)}) %all-gather.24.cloned.1.call-update) | async-done | bytes 2097168 | tf_op jit(solution)/shard_map/all_gather | solution.py:239
  439.1 22.1 %all-gather.28.cloned.1.call-done = bf16[1024,1152]{1,0:T(8,128)(2,1)} async-done(((bf16[128,1152]{1,0:T(8,128)(2,1)}), bf16[1024,1152]{1,0:T(8,128)(2,1)}) %all-gather.28.cloned.1.call-update) | async-done | bytes 2359312 | tf_op jit(solution)/shard_map/all_gather | solution.py:67
  468.6 40.3 %all-gather.44.cloned.1.call-done = bf16[1,1024,1024]{2,1,0:T(8,128)(2,1)} async-done(((bf16[1,256,1024]{2,1,0:T(8,128)(2,1)}), bf16[1,1024,1024]{2,1,0:T(8,128)(2,1)}) %all-gather.44.cloned.1.call-update) | async-done | bytes 2097168 | tf_op jit(solution)/shard_map/all_gather | solution.py:263
  508.9 29.9 %all-gather.30.cloned.1.call-done = bf16[1152,1024]{1,0:T(8,128)(2,1)} async-done(((bf16[1152,128]{1,0:T(8,128)(2,1)}), bf16[1152,1024]{1,0:T(8,128)(2,1)}) %all-gather.30.cloned.1.call-update) | async-done | bytes 2359312 | tf_op jit(solution)/shard_map/all_gather | solution.py:68
  538.8 10.8 multiply_convert_fusion.2
  557.4 49.3 %all-gather.38.cloned.1.call-done = bf16[1024,1024]{1,0:T(8,128)(2,1)} async-done(((bf16[256,1024]{1,0:T(8,128)(2,1)}), bf16[1024,1024]{1,0:T(8,128)(2,1)}) %all-gather.38.cloned.1.call-update) | async-done | bytes 2097168 | tf_op jit(solution)/shard_map/all_gather | solution.py:239
  618.6 36.3 %all-gather.46.cloned.1.call-done = bf16[1,1024,1024]{2,1,0:T(8,128)(2,1)} async-done(((bf16[1,256,1024]{2,1,0:T(8,128)(2,1)}), bf16[1,1024,1024]{2,1,0:T(8,128)(2,1)}) %all-gather.46.cloned.1.call-update) | async-done | bytes 2097168 | tf_op jit(solution)/shard_map/all_gather | solution.py:263
  654.9 10.9 multiply_convert_fusion
  680.7 35.6 %reduce-scatter.36.cloned.1.call-done = bf16[256,1024]{1,0:T(8,128)(2,1)} async-done(((bf16[1024,1024]{1,0:T(8,128)(2,1)}), bf16[256,1024]{1,0:T(8,128)(2,1)}) %reduce-scatter.36.cloned.1.call-update) | async-done | bytes 524304 | tf_op jit(solution)/shard_map/reduce_scatter | solution.py:272
  719.1 42.7 %reduce-scatter.26.cloned.1.call-done = bf16[256,1024]{1,0:T(8,128)(2,1)} async-done(((bf16[1024,1024]{1,0:T(8,128)(2,1)}), bf16[256,1024]{1,0:T(8,128)(2,1)}) %reduce-scatter.26.cloned.1.call-update) | async-done | bytes 524304 | tf_op jit(solution)/shard_map/reduce_scatter | solution.py:245
  767.1 43.3 %all-gather.40.cloned.1.call-done = bf16[1024,1024]{1,0:T(8,128)(2,1)} async-done(((bf16[256,1024]{1,0:T(8,128)(2,1)}), bf16[1024,1024]{1,0:T(8,128)(2,1)}) %all-gather.40.cloned.1.call-update) | async-done | bytes 2097168 | tf_op jit(solution)/shard_map/all_gather | solution.py:282
  815.4 35.1 %while.30 = (s32[]{:T(128)}, f32[1024,2,2,64]{0,3,2,1:T(8,128)S(1)}, bf16[4096,2,64]{0,2,1:T(8,128)(2,1)}, bf16[4096,2,64]{0,2,1:T(8,128)(2,1)}, s32[]{:T(128)},...) while((s32[]{:T(128)}, ...), condition=%wide.region_23.24_spmd.clone, body=%wide.region_22.23_spmd.clone.sunk | while | flops 2728003584 | bytes 93126936 | solution.py:155
  815.4 9.3 fusion.318
  825.4 9.2 fusion.319
  842.1 8.4 fusion.322
  862.6 34.7 %while.31 = (s32[]{:T(128)}, f32[1024,2,2,64]{0,3,2,1:T(8,128)S(1)}, bf16[4096,2,64]{0,2,1:T(8,128)(2,1)}, bf16[4096,2,64]{0,2,1:T(8,128)(2,1)}, s32[]{:T(128)},...) while((s32[]{:T(128)}, ...), condition=%wide.region_33.34_spmd.clone, body=%wide.region_32.33_spmd.clone.sunk | while | flops 2728003584 | bytes 99418456 | solution.py:155
  862.8 9.2 fusion.333
  872.7 9.5 fusion.334
  888.7 8.6 fusion.337
  910.4 68.9 %reduce-scatter.30.cloned.1.call-done = bf16[1024,2,64]{0,2,1:T(8,128)(2,1)} async-done(((bf16[4096,2,64]{0,2,1:T(8,128)(2,1)}), bf16[1024,2,64]{0,2,1:T(8,128)(2,1)}) %reduce-scatter.30.cloned.1.call-update) | async-done | bytes 262160 | tf_op jit(solution)/shard_map/reduce_scatter | solution.py:297
  980.5 142.9 %reduce-scatter.38.cloned.1.call-done = bf16[1024,2,64]{0,2,1:T(8,128)(2,1)} async-done(((bf16[4096,2,64]{0,2,1:T(8,128)(2,1)}), bf16[1024,2,64]{0,2,1:T(8,128)(2,1)}) %reduce-scatter.38.cloned.1.call-update) | async-done | bytes 262160 | tf_op jit(solution)/shard_map/reduce_scatter | solution.py:297
  1130.6 20.8 %reduce-scatter.32.cloned.1.call-done = bf16[1024,2,64]{0,2,1:T(8,128)(2,1)} async-done(((bf16[4096,2,64]{0,2,1:T(8,128)(2,1)}), bf16[1024,2,64]{0,2,1:T(8,128)(2,1)}) %reduce-scatter.32.cloned.1.call-update) | async-done | bytes 262160 | tf_op jit(solution)/shard_map/reduce_scatter | solution.py:300
  1162.8 16.0 reduce-scatter.40.cloned.1.call-done
  1238.9 31.9 %reduce-scatter.42.cloned.1.call-done = bf16[256,1024]{1,0:T(8,128)(2,1)} async-done(((bf16[1024,1024]{1,0:T(8,128)(2,1)}), bf16[256,1024]{1,0:T(8,128)(2,1)}) %reduce-scatter.42.cloned.1.call-update) | async-done | bytes 524304 | tf_op jit(solution)/shard_map/reduce_scatter | solution.py:316
  1273.0 43.3 %reduce-scatter.22.cloned.1.call-done = bf16[256,1024]{1,0:T(8,128)(2,1)} async-done(((bf16[1024,1024]{1,0:T(8,128)(2,1)}), bf16[256,1024]{1,0:T(8,128)(2,1)}) %reduce-scatter.22.cloned.1.call-update) | async-done | bytes 524304 | tf_op jit(solution)/shard_map/reduce_scatter | solution.py:245
  1319.6 39.9 %all-reduce.8 = (f32[1024]{0:T(1024)}, f32[1024]{0:T(1024)}, f32[64]{0:T(128)}, f32[64]{0:T(128)}) all-reduce(f32[1024]{0:T(1024)S(1)} %add.369, f32[1024]{0:T(1024)S(1)} %add.370, f32[64]{0:T(128)S(1)} %add.371, f32[64]{0:T(128)S(1)} %add.372), channel_id=1, replica_groups=mesh['shard'=2,'ctx'=4,'tp'=4] {'shard','ctx','tp'}, use_global_device_ids=true, to_apply=%region_49.50 | all-reduce | flops 2176 | bytes 17408 | tf_op jit(solution)/shard_map/psum | solution.py:337
  1365.2 9.0 reduce-scatter.52.cloned.1.call-done
  1374.2 58.2 %reduce-scatter.54.cloned.1.call-done = f32[128,1152]{1,0:T(8,128)} async-done(((f32[1024,1152]{1,0:T(8,128)}), f32[128,1152]{1,0:T(8,128)}) %reduce-scatter.54.cloned.1.call-update) | async-done | bytes 589840 | tf_op jit(solution)/shard_map/reduce_scatter | solution.py:334
  1432.3 57.9 %reduce-scatter.56.cloned.1.call-done = f32[1152,128]{1,0:T(8,128)} async-done(((f32[1152,1024]{1,0:T(8,128)}), f32[1152,128]{1,0:T(8,128)}) %reduce-scatter.56.cloned.1.call-update) | async-done | bytes 589840 | tf_op jit(solution)/shard_map/reduce_scatter | solution.py:335
  1490.3 40.1 %reduce-scatter.44.cloned.1.call-done = f32[128,256]{1,0:T(8,128)} async-done(((f32[1024,256]{1,0:T(8,128)}), f32[128,256]{1,0:T(8,128)}) %reduce-scatter.44.cloned.1.call-update) | async-done | bytes 131088 | tf_op jit(solution)/shard_map/reduce_scatter | solution.py:329
  1530.4 40.1 %reduce-scatter.50.cloned.1.call-done = f32[256,128]{1,0:T(8,128)} async-done(((f32[256,1024]{1,0:T(8,128)}), f32[256,128]{1,0:T(8,128)}) %reduce-scatter.50.cloned.1.call-update) | async-done | bytes 131088 | tf_op jit(solution)/shard_map/reduce_scatter | solution.py:332
  1570.5 37.9 %reduce-scatter.46.cloned.1.call-done = f32[128,128]{1,0:T(8,128)} async-done(((f32[1024,128]{1,0:T(8,128)}), f32[128,128]{1,0:T(8,128)}) %reduce-scatter.46.cloned.1.call-update) | async-done | bytes 65552 | tf_op jit(solution)/shard_map/reduce_scatter | solution.py:330
  1608.5 37.7 %reduce-scatter.48.cloned.1.call-done = f32[128,128]{1,0:T(8,128)} async-done(((f32[1024,128]{1,0:T(8,128)}), f32[128,128]{1,0:T(8,128)}) %reduce-scatter.48.cloned.1.call-update) | async-done | bytes 65552 | tf_op jit(solution)/shard_map/reduce_scatter | solution.py:331
  (477 shorter events, 256.3 us)
Async XLA Ops:
  8.0 54.0 %all-gather.18.cloned.1.call-start = ((), (), s32[]{:S(2)}) async-start(), calls=%async_computation.19 | async-start | bytes 2621440 | tf_op jit(solution)/shard_map/all_gather | solution.py:204
  13.3 95.5 %all-gather.32.cloned.1.call-start = ((), (), s32[]{:S(2)}) async-start(), calls=%async_computation.28 | async-start | bytes 2621440 | tf_op jit(solution)/shard_map/all_gather | solution.py:204
  14.0 150.3 %all-gather.20.cloned.1.call-start = ((), (), s32[]{:S(2)}) async-start(), calls=%async_computation.20 | async-start | bytes 1310720 | tf_op jit(solution)/shard_map/all_gather | solution.py:82
  113.9 50.4 %all-gather.22.cloned.1.call-start = ((), (), s32[]{:S(2)}) async-start(), calls=%async_computation.21 | async-start | bytes 1310720 | tf_op jit(solution)/shard_map/all_gather | solution.py:83
  125.2 127.7 %all-gather.34.cloned.1.call-start = ((), (), s32[]{:S(2)}) async-start(), calls=%async_computation.29 | async-start | bytes 1310720 | tf_op jit(solution)/shard_map/all_gather | solution.py:82
  140.2 112.7 %all-gather.36.cloned.1.call-start = ((), (), s32[]{:S(2)}) async-start(), calls=%async_computation.30 | async-start | bytes 1310720 | tf_op jit(solution)/shard_map/all_gather | solution.py:83
  156.7 183.3 %reduce-scatter.20.cloned.1.call-start = ((), (), s32[]{:S(2)}) async-start(), calls=%async_computation.22 | async-start | bytes 2621440 | tf_op jit(solution)/shard_map/reduce_scatter | solution.py:231
  252.6 129.7 %reduce-scatter.24.cloned.1.call-start = ((), (), s32[]{:S(2)}) async-start(), calls=%async_computation.31 | async-start | bytes 2621440 | tf_op jit(solution)/shard_map/reduce_scatter | solution.py:231
  339.4 51.6 %all-gather.26.cloned.1.call-start = ((), (), s32[]{:S(2)}) async-start(), calls=%async_computation.24 | async-start | bytes 2654208 | tf_op jit(solution)/shard_map/all_gather | solution.py:66
  340.0 91.8 %all-gather.24.cloned.1.call-start = ((), (), s32[]{:S(2)}) async-start(), calls=%async_computation.23 | async-start | bytes 2621440 | tf_op jit(solution)/shard_map/all_gather | solution.py:239
  384.0 377.8 %copy-start.96 = (f32[256]{0:T(256)}, f32[256]{0:T(256)S(1)}, u32[]{:S(2)}) copy-start(f32[256]{0:T(256)S(1)} %fusion.156) | copy-start | bytes 3076
  384.0 377.8 %copy-start.94 = (f32[256]{0:T(256)}, f32[256]{0:T(256)S(1)}, u32[]{:S(2)}) copy-start(f32[256]{0:T(256)S(1)} %fusion.158) | copy-start | bytes 3076
  386.7 74.4 %all-gather.28.cloned.1.call-start = ((), (), s32[]{:S(2)}) async-start(), calls=%async_computation.25 | async-start | bytes 2654208 | tf_op jit(solution)/shard_map/all_gather | solution.py:67
  387.3 121.6 %all-gather.44.cloned.1.call-start = ((), (), s32[]{:S(2)}) async-start(), calls=%async_computation.51 | async-start | bytes 2621440 | tf_op jit(solution)/shard_map/all_gather | solution.py:263
  388.4 150.4 %all-gather.30.cloned.1.call-start = ((), (), s32[]{:S(2)}) async-start(), calls=%async_computation.26 | async-start | bytes 2654208 | tf_op jit(solution)/shard_map/all_gather | solution.py:68
  389.2 217.5 %all-gather.38.cloned.1.call-start = ((), (), s32[]{:S(2)}) async-start(), calls=%async_computation.32 | async-start | bytes 2621440 | tf_op jit(solution)/shard_map/all_gather | solution.py:239
  389.9 265.0 %all-gather.46.cloned.1.call-start = ((), (), s32[]{:S(2)}) async-start(), calls=%async_computation.52 | async-start | bytes 2621440 | tf_op jit(solution)/shard_map/all_gather | solution.py:263
  390.5 290.2 %reduce-scatter.28.cloned.1.call-start = ((), (), s32[]{:S(2)}) async-start(), calls=%async_computation.34 | async-start | bytes 2621440 | tf_op jit(solution)/shard_map/reduce_scatter | solution.py:272
  557.1 159.1 %reduce-scatter.36.cloned.1.call-start = ((), (), s32[]{:S(2)}) async-start(), calls=%async_computation.39 | async-start | bytes 2621440 | tf_op jit(solution)/shard_map/reduce_scatter | solution.py:272
  673.4 88.4 %reduce-scatter.26.cloned.1.call-start = ((), (), s32[]{:S(2)}) async-start(), calls=%async_computation.33 | async-start | bytes 2621440 | tf_op jit(solution)/shard_map/reduce_scatter | solution.py:245
  680.2 130.2 %all-gather.40.cloned.1.call-start = ((), (), s32[]{:S(2)}) async-start(), calls=%async_computation.35 | async-start | bytes 2621440 | tf_op jit(solution)/shard_map/all_gather | solution.py:282
  765.4 91.4 %all-gather.42.cloned.1.call-start = ((), (), s32[]{:S(2)}) async-start(), calls=%async_computation.40 | async-start | bytes 2621440 | tf_op jit(solution)/shard_map/all_gather | solution.py:282
  767.0 212.3 %reduce-scatter.30.cloned.1.call-start = ((), (), s32[]{:S(2)}) async-start(), calls=%async_computation.36 | async-start | bytes 1310720 | tf_op jit(solution)/shard_map/reduce_scatter | solution.py:297
  850.6 272.8 %reduce-scatter.38.cloned.1.call-start = ((), (), s32[]{:S(2)}) async-start(), calls=%async_computation.41 | async-start | bytes 1310720 | tf_op jit(solution)/shard_map/reduce_scatter | solution.py:297
  897.3 254.2 %reduce-scatter.32.cloned.1.call-start = ((), (), s32[]{:S(2)}) async-start(), calls=%async_computation.37 | async-start | bytes 1310720 | tf_op jit(solution)/shard_map/reduce_scatter | solution.py:300
  900.8 278.0 %reduce-scatter.40.cloned.1.call-start = ((), (), s32[]{:S(2)}) async-start(), calls=%async_computation.42 | async-start | bytes 1310720 | tf_op jit(solution)/shard_map/reduce_scatter | solution.py:300
  907.5 215.9 %copy-start.46 = (f32[1024,64]{0,1:T(8,128)S(1)}, f32[1024,64]{0,1:T(8,128)}, u32[]{:S(2)}) copy-start(f32[1024,64]{0,1:T(8,128)} %copy-done.45) | copy-start | bytes 786436
  907.5 217.1 %copy-start.18 = (f32[1024,128]{0,1:T(8,128)S(1)}, f32[1024,128]{0,1:T(8,128)}, u32[]{:S(2)}) copy-start(f32[1024,128]{0,1:T(8,128)} %copy-done.17) | copy-start | bytes 1572868
  907.5 217.1 %copy-start.20 = (f32[1024,128]{0,1:T(8,128)S(1)}, f32[1024,128]{0,1:T(8,128)}, u32[]{:S(2)}) copy-start(f32[1024,128]{0,1:T(8,128)} %copy-done.19) | copy-start | bytes 1572868
  907.5 217.1 %copy-start.31 = (f32[1024,64]{0,1:T(8,128)S(1)}, f32[1024,64]{0,1:T(8,128)}, u32[]{:S(2)}) copy-start(f32[1024,64]{0,1:T(8,128)} %copy-done.28) | copy-start | bytes 786436
  907.5 217.1 %copy-start.81 = (f32[1024,2]{0,1:T(2,128)S(1)}, f32[1024,2]{0,1:T(2,128)}, u32[]{:S(2)}) copy-start(f32[1024,2]{0,1:T(2,128)} %copy-done.80) | copy-start | bytes 24580
  907.5 217.1 %copy-start.83 = (f32[1024,2]{0,1:T(2,128)S(1)}, f32[1024,2]{0,1:T(2,128)}, u32[]{:S(2)}) copy-start(f32[1024,2]{0,1:T(2,128)} %copy-done.82) | copy-start | bytes 24580
  907.5 217.1 %copy-start.116 = (f32[64]{0:T(128)S(1)}, f32[64]{0:T(128)}, u32[]{:S(2)}) copy-start(f32[64]{0:T(128)} %param.29) | copy-start | bytes 772
  910.4 215.8 %copy-start.87 = (f32[1024,2]{0,1:T(2,128)S(1)}, f32[1024,2]{0,1:T(2,128)}, u32[]{:S(2)}) copy-start(f32[1024,2]{0,1:T(2,128)} %copy-done.86) | copy-start | bytes 24580
  910.4 215.9 %copy-start.89 = (f32[1024,2]{0,1:T(2,128)S(1)}, f32[1024,2]{0,1:T(2,128)}, u32[]{:S(2)}) copy-start(f32[1024,2]{0,1:T(2,128)} %copy-done.88) | copy-start | bytes 24580
  910.4 328.5 %reduce-scatter.34.cloned.1.call-start = ((), (), s32[]{:S(2)}) async-start(), calls=%async_computation.38 | async-start | bytes 2621440 | tf_op jit(solution)/shard_map/reduce_scatter | solution.py:316
  979.4 145.3 %copy-start.65 = (bf16[1024,2,64]{0,2,1:T(8,128)(2,1)S(1)}, bf16[1024,2,64]{0,2,1:T(8,128)(2,1)}, u32[]{:S(2)}) copy-start(bf16[1024,2,64]{0,2,1:T(8,128)(2,1)} %reduce-scatter.30.cloned.1.call-done) | copy-start | bytes 786436
  980.5 145.8 %copy-start.67 = (f32[1024,2,32]{0,2,1:T(8,128)}, f32[1024,2,32]{0,2,1:T(8,128)S(1)}, u32[]{:S(2)}) copy-start(f32[1024,2,32]{0,2,1:T(8,128)S(1)} %get-tuple-element.358) | copy-start | bytes 786436
  980.5 145.8 %copy-start.68 = (f32[1024,2,32]{0,2,1:T(8,128)}, f32[1024,2,32]{0,2,1:T(8,128)S(1)}, u32[]{:S(2)}) copy-start(f32[1024,2,32]{0,2,1:T(8,128)S(1)} %get-tuple-element.359) | copy-start | bytes 786436
  1157.2 113.7 %reduce-scatter.42.cloned.1.call-start = ((), (), s32[]{:S(2)}) async-start(), calls=%async_computation.43 | async-start | bytes 2621440 | tf_op jit(solution)/shard_map/reduce_scatter | solution.py:316
  1184.4 131.9 %reduce-scatter.22.cloned.1.call-start = ((), (), s32[]{:S(2)}) async-start(), calls=%async_computation.27 | async-start | bytes 2621440 | tf_op jit(solution)/shard_map/reduce_scatter | solution.py:245
  1191.2 183.0 %reduce-scatter.52.cloned.1.call-start = ((), (), s32[]{:S(2)}) async-start(), calls=%async_computation.48 | async-start | bytes 5308416 | tf_op jit(solution)/shard_map/reduce_scatter | solution.py:333
  1201.3 231.0 %reduce-scatter.54.cloned.1.call-start = ((), (), s32[]{:S(2)}) async-start(), calls=%async_computation.49 | async-start | bytes 5308416 | tf_op jit(solution)/shard_map/reduce_scatter | solution.py:334
  1211.0 279.3 %reduce-scatter.56.cloned.1.call-start = ((), (), s32[]{:S(2)}) async-start(), calls=%async_computation.50 | async-start | bytes 5308416 | tf_op jit(solution)/shard_map/reduce_scatter | solution.py:335
  1221.4 309.0 %reduce-scatter.44.cloned.1.call-start = ((), (), s32[]{:S(2)}) async-start(), calls=%async_computation.44 | async-start | bytes 1179648 | tf_op jit(solution)/shard_map/reduce_scatter | solution.py:329
  1227.6 342.9 %reduce-scatter.50.cloned.1.call-start = ((), (), s32[]{:S(2)}) async-start(), calls=%async_computation.47 | async-start | bytes 1179648 | tf_op jit(solution)/shard_map/reduce_scatter | solution.py:332
  1231.9 376.6 %reduce-scatter.46.cloned.1.call-start = ((), (), s32[]{:S(2)}) async-start(), calls=%async_computation.45 | async-start | bytes 589824 | tf_op jit(solution)/shard_map/reduce_scatter | solution.py:330
  1235.5 410.7 %reduce-scatter.48.cloned.1.call-start = ((), (), s32[]{:S(2)}) async-start(), calls=%async_computation.46 | async-start | bytes 589824 | tf_op jit(solution)/shard_map/reduce_scatter | solution.py:331
  (123 other events, 2753.7 us)
Sparse Core Ops, SparseCore 0:
  13.4 48.6 all-gather.17
  64.2 44.5 all-gather.31
  114.1 15.5 all-gather.19
  131.7 17.8 all-gather.21
  151.0 17.9 all-gather.33
  170.4 16.7 all-gather.35
  252.7 42.6 reduce-scatter.19
  339.5 42.7 reduce-scatter.23
  557.2 63.3 reduce-scatter.27
  673.6 42.6 reduce-scatter.35
  718.6 43.1 reduce-scatter.25
  850.7 128.6 reduce-scatter.29
  981.9 141.4 reduce-scatter.37
  1126.5 24.8 reduce-scatter.31
  1153.8 24.8 reduce-scatter.39
  1181.6 43.8 reduce-scatter.33
  1227.6 43.1 reduce-scatter.41
  1273.1 43.1 reduce-scatter.21
  1320.3 53.8 reduce-scatter.51
  1378.4 53.8 reduce-scatter.53
  1436.4 53.8 reduce-scatter.55
  1494.3 36.0 reduce-scatter.43
  1534.5 35.9 reduce-scatter.49
  1574.3 34.0 reduce-scatter.45
  1612.1 34.0 reduce-scatter.47
Sparse Core Ops, SparseCore 1:
  341.7 27.7 all-gather.25
  386.8 44.9 all-gather.23
  433.5 27.6 all-gather.27
  463.3 45.5 all-gather.43
  510.8 28.0 all-gather.29
  541.1 65.5 all-gather.37
  608.1 46.7 all-gather.45
  765.5 44.8 all-gather.39
  812.4 44.3 all-gather.41
where the time goes:
time: 1660 us; the launch traced here: 1650 us
  waiting for transfers between devices  1080 us (65%)
  matrix products  331 us (20%)
  other arithmetic  120 us (7%)
  blocking collectives  83.1 us (5%)
  local copies, waits for them, and re-layouts  20 us (1%)
  between operations  17.8 us (1%)
    reduce_scatter x2, waiting for transfers between devices, per_device(): lax.psum_scatter(key_buffer.astype(jnp.bfloat16), 'ctx', scatter_dimensio...  212 us
    all_gather x2, waiting for transfers between devices, per_device(): second_all = lax.all_gather(second, 'tp', axis=0, tiled=True)  90 us
    reduce_scatter x2, waiting for transfers between devices, per_device(): lax.psum_scatter(project_rows(hidden_b, down_full).astype(jnp.bfloat16),...  86 us
    all_gather x2, waiting for transfers between devices, per_device(): first_all = lax.all_gather(first, 'tp', axis=0, tiled=True)  79.1 us
    all_gather x2, waiting for transfers between devices, per_device(): upstream_all = lax.all_gather(upstream_b, 'tp', axis=0, tiled=True)  76.7 us
    dot_general x14, matrix products, dot_last(): lax.dot_general(left, right, (((1,), (1,)), ((), ())), preferred_element_...  64.4 us
    reduce_scatter x1, waiting for transfers between devices, per_device(): lax.psum_scatter(up_acc, ('shard', 'ctx'), scatter_dimension=0, tiled=True)  58.2 us
    reduce_scatter x1, waiting for transfers between devices, per_device(): lax.psum_scatter(down_acc, ('shard', 'ctx'), scatter_dimension=1, tiled=T...  57.9 us
  transfers between devices with their start and end apart: 34, of which 26 were waited for; matrix products, arithmetic and copies ran while one was open for 27% of the time, Pallas kernels for 0%

commit v1 on v0

--- a/solution.py
+++ b/solution.py
@@ -7,6 +7,27 @@
 EPS = 1e-05
 THETA = 1000000.0
 NEGATIVE = -1e30
+
+
+def see_blocks(w_in, in_dim):
+    near = list(w_in.shape[1:])
+    near[in_dim] *= w_in.shape[0]
+    return jnp.moveaxis(w_in, 0, in_dim).reshape(near)
+
+
+def put_the_view(vals, shard_axis):
+    n_all = lax.axis_size(shard_axis)
+    heard = vals[None]
+    for j in range(n_all.bit_length() - 1):
+        p_next = 1 << j
+        b_next = lax.ppermute(
+            heard, shard_axis, list(map(lambda j0: (j0, j0 ^ p_next), range(n_all)))
+        )
+        earlier = jnp.stack([heard, b_next])
+        k_now = lax.axis_index(shard_axis)
+        v_next = k_now >> j & 1
+        heard = jnp.where(v_next == 0, earlier, earlier[::-1]).reshape(-1, *vals.shape)
+    return heard
 
 
 def norm_rows(values, gain):
@@ -201,7 +222,8 @@
         query_full, key_full, value_full, output_full, gate_full, up_full, down_full = current
         token_rows = tokens[seq].astype(jnp.float32)
         first = norm_rows(token_rows, first_gain).astype(jnp.bfloat16)
-        first_all = lax.all_gather(first, "tp", axis=0, tiled=True)
+        a_next = put_the_view(first, "tp")
+        first_all = see_blocks(a_next, 0)
         cosine, sine = rotary_tables(positions[seq], head_dim)
         query_raw = jnp.dot(first_all, query_full, preferred_element_type=jnp.float32).reshape(
             span_rows, -1, head_dim

time: 1660 us -> 1700 us (1.024)
    ppermute x0 -> x4, waiting for transfers between devices: none -> 83.2 us  [put_the_view(): lax.ppermute(heard, shard_axis, list(map(lambda j0: (j0, j0 ^ p_next), ra...]
    all_gather x2 -> x0, waiting for transfers between devices: 79.1 us -> none  [per_device(): first_all = lax.all_gather(first, 'tp', axis=0, tiled=True)]
  transfers between devices with their start and end apart: 34 -> 36, of which waited for: 26 -> 28; matrix products, arithmetic and copies ran while one was open for 27% -> 27% of each run, Pallas kernels for 0% -> 0%
where the time goes in v1:
time: 1700 us; the launch traced here: 1690 us
  waiting for transfers between devices  1090 us (64%)
  matrix products  335 us (20%)
  other arithmetic  122 us (7%)
  blocking collectives  80.3 us (5%)
  local copies, waits for them, and re-layouts  21.7 us (1%)
  starting transfers between devices  20.3 us (1%)
  between operations  17.7 us (1%)
    reduce_scatter x2, waiting for transfers between devices, per_device(): lax.psum_scatter(key_buffer.astype(jnp.bfloat16), 'ctx', scatter_dimensio...  222 us
    reduce_scatter x2, waiting for transfers between devices, per_device(): lax.psum_scatter(project_rows(hidden_b, down_full).astype(jnp.bfloat16),...  86 us
    all_gather x2, waiting for transfers between devices, per_device(): upstream_all = lax.all_gather(upstream_b, 'tp', axis=0, tiled=True)  83.6 us
    ppermute x4, waiting for transfers between devices, put_the_view(): lax.ppermute(heard, shard_axis, list(map(lambda j0: (j0, j0 ^ p_next), ra...  83.2 us
    all_gather x2, waiting for transfers between devices, per_device(): second_all = lax.all_gather(second, 'tp', axis=0, tiled=True)  80.8 us
    dot_general x14, matrix products, dot_last(): lax.dot_general(left, right, (((1,), (1,)), ((), ())), preferred_element_...  64.4 us
    reduce_scatter x1, waiting for transfers between devices, per_device(): lax.psum_scatter(up_acc, ('shard', 'ctx'), scatter_dimension=0, tiled=True)  58.2 us
    reduce_scatter x1, waiting for transfers between devices, per_device(): lax.psum_scatter(down_acc, ('shard', 'ctx'), scatter_dimension=1, tiled=T...  57.9 us
  transfers between devices with their start and end apart: 36, of which 28 were waited for; matrix products, arithmetic and copies ran while one was open for 27% of the time, Pallas kernels for 0%

profile of v1, /device:TPU:0, one launch (start us, length us, event | category | flops | bytes accessed | tf_op | source)
XLA Modules:
  0.0 1686.3 jit_solution(11471679756842796130)
XLA Ops:
  17.2 10.4 collective-permute-done
  33.1 13.9 collective-permute-done.2
  49.6 9.6 all_gather.34
  59.3 42.0 %collective-permute-done.1 = bf16[2,256,1024]{2,1,0:T(8,128)(2,1)} collective-permute-done((bf16[2,256,1024]{2,1,0:T(8,128)(2,1)}, bf16[2,256,1024]{2,1,0:T(8,128)(2,1)}, u32[]{:S(2)}, u32[]{:S(2)}) %collective-permute-start.1) | collective-permute-done | bytes 1048608 | tf_op jit(solution)/shard_map/ppermute | solution.py:23
  104.3 16.8 collective-permute-done.3
  126.1 9.2 all_gather.37
  141.9 9.8 all_gather.36
  152.7 11.8 all_gather.39
  171.9 10.8 reduce-scatter.20.cloned.1.call-start
  186.0 84.7 %conditional.2 = (f32[2,2,1024]{2,1,0:T(2,128)}, f32[2,2,1024]{2,1,0:T(2,128)}, f32[2,2,1024,64]{2,3,1,0:T(8,128)S(1)}, f32[2,2,1024]{2,1,0:T(2,128)S(1)}) conditional(s32[]{:T(128)} %convert_element_type.314, () %tuple.36, (s32[1024]{0:T(1024)S(1)}, bf16[4096,2,64]{0,2,1:T(8,128)(2,1)}, bf16[1024,2,2,64]{0,3,2,1:T(8,128)(2,1)}, ...), branch_computations={%region_3.4_spmd, %region_4.7_spmd} | conditional | flops 4517261312 | bytes 221909024 | solution.py:126
  191.8 27.3 %fusion.4 = (f32[2,2,1024]{2,1,0:T(2,128)S(1)}, f32[2,4096,1024,2]{2,1,3,0:T(8,128)}) fusion(pred[1024,4096]{0,1:T(8,128)(4,1)} %iota_compare_fusion, bf16[1024,2,2,64]{0,3,2,1:T(8,128)(2,1)} %get-tuple-element.116, bf16[4096,2,64]{0,2,1:T(8,128)(2,1)} %get-tuple-element.115), kind=kOutput, calls=%fused_computation.4 | convolution fusion | flops 2197811200 | bytes 72892416 | tf_op jit(solution)/shard_map/cond/branch_1_fun/qkgd,nkd->kgqn/dot_general | solution.py:109
  219.7 23.8 %fusion.6 = f32[2,2,1024]{2,1,0:T(2,128)} fusion(f32[2,4096,1024,2]{2,1,3,0:T(8,128)} %get-tuple-element.326, f32[2,2,1024]{2,1,0:T(2,128)} %broadcast_maximum_fusion, pred[1024,4096]{0,1:T(8,128)(4,1)} %iota_compare_fusion), kind=kLoop, calls=%fused_computation.6 | loop fusion | flops 83881984 | bytes 71335936 | tf_op jit(solution)/shard_map/cond/branch_1_fun/reduce_sum | solution.py:117
  243.5 26.4 %fusion.7 = f32[2,2,1024,64]{2,3,1,0:T(8,128)S(1)} fusion(f32[2,4096,1024,2]{2,1,3,0:T(8,128)} %get-tuple-element.326, f32[2,2,1024]{2,1,0:T(2,128)} %broadcast_maximum_fusion, pred[1024,4096]{0,1:T(8,128)(4,1)} %iota_compare_fusion, bf16[4096,2,64]{0,2,1:T(8,128)(2,1)} %get-tuple-element.117), kind=kOutput, calls=%fused_computation.7 | convolution fusion | flops 2231369728 | bytes 73416704 | tf_op jit(solution)/shard_map/cond/branch_1_fun/kgqn,nkd->kgqd/dot_general | solution.py:118
  276.8 83.5 %conditional.3 = (f32[2,2,1024]{2,1,0:T(2,128)}, f32[2,2,1024]{2,1,0:T(2,128)}, f32[2,2,1024,64]{2,3,1,0:T(8,128)S(1)}, f32[2,2,1024]{2,1,0:T(2,128)S(1)}) conditional(s32[]{:T(128)} %convert_element_type.314, () %tuple.38, (s32[1024]{0:T(1024)S(1)}, bf16[4096,2,64]{0,2,1:T(8,128)(2,1)}, bf16[1024,2,2,64]{0,3,2,1:T(8,128)(2,1)}, ...), branch_computations={%region_13.14_spmd, %region_14.17_spmd} | conditional | flops 4517261312 | bytes 230297696 | solution.py:126
  282.6 26.1 %fusion.16 = (f32[2,2,1024]{2,1,0:T(2,128)S(1)}, f32[2,4096,1024,2]{2,1,3,0:T(8,128)}) fusion(pred[1024,4096]{0,1:T(8,128)(4,1)} %iota_compare_fusion.1, bf16[1024,2,2,64]{0,3,2,1:T(8,128)(2,1)} %get-tuple-element.120, bf16[4096,2,64]{0,2,1:T(8,128)(2,1)S(1)} %copy-done.25), kind=kOutput, calls=%fused_computation.19 | convolution fusion | flops 2197811200 | bytes 72892416 | tf_op jit(solution)/shard_map/cond/branch_1_fun/qkgd,nkd->kgqn/dot_general | solution.py:109
  309.3 24.1 %fusion.18 = f32[2,2,1024]{2,1,0:T(2,128)} fusion(f32[2,4096,1024,2]{2,1,3,0:T(8,128)} %get-tuple-element.328, f32[2,2,1024]{2,1,0:T(2,128)} %broadcast_maximum_fusion.1, pred[1024,4096]{0,1:T(8,128)(4,1)} %iota_compare_fusion.1), kind=kLoop, calls=%fused_computation.21 | loop fusion | flops 83881984 | bytes 71335936 | tf_op jit(solution)/shard_map/cond/branch_1_fun/reduce_sum | solution.py:117
  333.4 26.1 %fusion.19 = f32[2,2,1024,64]{2,3,1,0:T(8,128)S(1)} fusion(f32[2,4096,1024,2]{2,1,3,0:T(8,128)} %get-tuple-element.328, f32[2,2,1024]{2,1,0:T(2,128)} %broadcast_maximum_fusion.1, pred[1024,4096]{0,1:T(8,128)(4,1)} %iota_compare_fusion.1, bf16[4096,2,64]{0,2,1:T(8,128)(2,1)S(1)} %copy-done.115), kind=kOutput, calls=%fused_computation.22 | convolution fusion | flops 2231369728 | bytes 73416704 | tf_op jit(solution)/shard_map/cond/branch_1_fun/kgqn,nkd->kgqd/dot_general | solution.py:118
  364.7 43.4 %reduce-scatter.24.cloned.1.call-done = bf16[256,1024]{1,0:T(8,128)(2,1)} async-done(((bf16[1024,1024]{1,0:T(8,128)(2,1)}), bf16[256,1024]{1,0:T(8,128)(2,1)}) %reduce-scatter.24.cloned.1.call-update) | async-done | bytes 524304 | tf_op jit(solution)/shard_map/reduce_scatter | solution.py:253
  416.6 40.9 %all-gather.20.cloned.1.call-done = bf16[1024,1024]{1,0:T(8,128)(2,1)} async-done(((bf16[256,1024]{1,0:T(8,128)(2,1)}), bf16[1024,1024]{1,0:T(8,128)(2,1)}) %all-gather.20.cloned.1.call-update) | async-done | bytes 2097168 | tf_op jit(solution)/shard_map/all_gather | solution.py:261
  464.9 22.1 %all-gather.24.cloned.1.call-done = bf16[1024,1152]{1,0:T(8,128)(2,1)} async-done(((bf16[128,1152]{1,0:T(8,128)(2,1)}), bf16[1024,1152]{1,0:T(8,128)(2,1)}) %all-gather.24.cloned.1.call-update) | async-done | bytes 2359312 | tf_op jit(solution)/shard_map/all_gather | solution.py:88
  494.4 39.8 %all-gather.38.cloned.1.call-done = bf16[1,1024,1024]{2,1,0:T(8,128)(2,1)} async-done(((bf16[1,256,1024]{2,1,0:T(8,128)(2,1)}), bf16[1,1024,1024]{2,1,0:T(8,128)(2,1)}) %all-gather.38.cloned.1.call-update) | async-done | bytes 2097168 | tf_op jit(solution)/shard_map/all_gather | solution.py:285
  534.1 29.9 %all-gather.26.cloned.1.call-done = bf16[1152,1024]{1,0:T(8,128)(2,1)} async-done(((bf16[1152,128]{1,0:T(8,128)(2,1)}), bf16[1152,1024]{1,0:T(8,128)(2,1)}) %all-gather.26.cloned.1.call-update) | async-done | bytes 2359312 | tf_op jit(solution)/shard_map/all_gather | solution.py:89
  564.0 10.8 multiply_convert_fusion.2
  582.9 39.9 %all-gather.32.cloned.1.call-done = bf16[1024,1024]{1,0:T(8,128)(2,1)} async-done(((bf16[256,1024]{1,0:T(8,128)(2,1)}), bf16[1024,1024]{1,0:T(8,128)(2,1)}) %all-gather.32.cloned.1.call-update) | async-done | bytes 2097168 | tf_op jit(solution)/shard_map/all_gather | solution.py:261
  634.9 43.8 %all-gather.40.cloned.1.call-done = bf16[1,1024,1024]{2,1,0:T(8,128)(2,1)} async-done(((bf16[1,256,1024]{2,1,0:T(8,128)(2,1)}), bf16[1,1024,1024]{2,1,0:T(8,128)(2,1)}) %all-gather.40.cloned.1.call-update) | async-done | bytes 2097168 | tf_op jit(solution)/shard_map/all_gather | solution.py:285
  678.7 10.9 multiply_convert_fusion
  704.2 35.9 %reduce-scatter.36.cloned.1.call-done = bf16[256,1024]{1,0:T(8,128)(2,1)} async-done(((bf16[1024,1024]{1,0:T(8,128)(2,1)}), bf16[256,1024]{1,0:T(8,128)(2,1)}) %reduce-scatter.36.cloned.1.call-update) | async-done | bytes 524304 | tf_op jit(solution)/shard_map/reduce_scatter | solution.py:294
  742.9 42.7 %reduce-scatter.26.cloned.1.call-done = bf16[256,1024]{1,0:T(8,128)(2,1)} async-done(((bf16[1024,1024]{1,0:T(8,128)(2,1)}), bf16[256,1024]{1,0:T(8,128)(2,1)}) %reduce-scatter.26.cloned.1.call-update) | async-done | bytes 524304 | tf_op jit(solution)/shard_map/reduce_scatter | solution.py:267
  790.9 43.4 %all-gather.34.cloned.1.call-done = bf16[1024,1024]{1,0:T(8,128)(2,1)} async-done(((bf16[256,1024]{1,0:T(8,128)(2,1)}), bf16[1024,1024]{1,0:T(8,128)(2,1)}) %all-gather.34.cloned.1.call-update) | async-done | bytes 2097168 | tf_op jit(solution)/shard_map/all_gather | solution.py:304
  839.3 35.1 %while.30 = (s32[]{:T(128)}, f32[1024,2,2,64]{0,3,2,1:T(8,128)S(1)}, bf16[4096,2,64]{0,2,1:T(8,128)(2,1)}, bf16[4096,2,64]{0,2,1:T(8,128)(2,1)}, s32[]{:T(128)},...) while((s32[]{:T(128)}, ...), condition=%wide.region_23.24_spmd.clone, body=%wide.region_22.23_spmd.clone.sunk | while | flops 2728003584 | bytes 93126936 | solution.py:176
  839.3 9.3 fusion.339
  849.3 9.2 fusion.340
  886.0 37.1 %while.31 = (s32[]{:T(128)}, f32[1024,2,2,64]{0,3,2,1:T(8,128)S(1)}, bf16[4096,2,64]{0,2,1:T(8,128)(2,1)}, bf16[4096,2,64]{0,2,1:T(8,128)(2,1)}, s32[]{:T(128)},...) while((s32[]{:T(128)}, ...), condition=%wide.region_33.34_spmd.clone, body=%wide.region_32.33_spmd.clone.sunk | while | flops 2728003584 | bytes 95224120 | solution.py:176
  886.2 9.4 fusion.354
  913.0 10.1 fusion.358
  933.0 70.2 %reduce-scatter.30.cloned.1.call-done = bf16[1024,2,64]{0,2,1:T(8,128)(2,1)} async-done(((bf16[4096,2,64]{0,2,1:T(8,128)(2,1)}), bf16[1024,2,64]{0,2,1:T(8,128)(2,1)}) %reduce-scatter.30.cloned.1.call-update) | async-done | bytes 262160 | tf_op jit(solution)/shard_map/reduce_scatter | solution.py:319
  1005.0 152.0 %reduce-scatter.38.cloned.1.call-done = bf16[1024,2,64]{0,2,1:T(8,128)(2,1)} async-done(((bf16[4096,2,64]{0,2,1:T(8,128)(2,1)}), bf16[1024,2,64]{0,2,1:T(8,128)(2,1)}) %reduce-scatter.38.cloned.1.call-update) | async-done | bytes 262160 | tf_op jit(solution)/shard_map/reduce_scatter | solution.py:319
  1164.1 20.4 %reduce-scatter.32.cloned.1.call-done = bf16[1024,2,64]{0,2,1:T(8,128)(2,1)} async-done(((bf16[4096,2,64]{0,2,1:T(8,128)(2,1)}), bf16[1024,2,64]{0,2,1:T(8,128)(2,1)}) %reduce-scatter.32.cloned.1.call-update) | async-done | bytes 262160 | tf_op jit(solution)/shard_map/reduce_scatter | solution.py:322
  1195.8 16.2 reduce-scatter.40.cloned.1.call-done
  1271.7 31.8 %reduce-scatter.42.cloned.1.call-done = bf16[256,1024]{1,0:T(8,128)(2,1)} async-done(((bf16[1024,1024]{1,0:T(8,128)(2,1)}), bf16[256,1024]{1,0:T(8,128)(2,1)}) %reduce-scatter.42.cloned.1.call-update) | async-done | bytes 524304 | tf_op jit(solution)/shard_map/reduce_scatter | solution.py:338
  1305.6 43.3 %reduce-scatter.22.cloned.1.call-done = bf16[256,1024]{1,0:T(8,128)(2,1)} async-done(((bf16[1024,1024]{1,0:T(8,128)(2,1)}), bf16[256,1024]{1,0:T(8,128)(2,1)}) %reduce-scatter.22.cloned.1.call-update) | async-done | bytes 524304 | tf_op jit(solution)/shard_map/reduce_scatter | solution.py:267
  1352.2 39.9 %all-reduce.8 = (f32[1024]{0:T(1024)}, f32[1024]{0:T(1024)}, f32[64]{0:T(128)}, f32[64]{0:T(128)}) all-reduce(f32[1024]{0:T(1024)S(1)} %add.363, f32[1024]{0:T(1024)S(1)} %add.364, f32[64]{0:T(128)S(1)} %add.365, f32[64]{0:T(128)S(1)} %add.366), channel_id=1, replica_groups=mesh['shard'=2,'ctx'=4,'tp'=4] {'shard','ctx','tp'}, use_global_device_ids=true, to_apply=%region_49.50 | all-reduce | flops 2176 | bytes 17408 | tf_op jit(solution)/shard_map/psum | solution.py:359
  1406.7 58.2 %reduce-scatter.54.cloned.1.call-done = f32[128,1152]{1,0:T(8,128)} async-done(((f32[1024,1152]{1,0:T(8,128)}), f32[128,1152]{1,0:T(8,128)}) %reduce-scatter.54.cloned.1.call-update) | async-done | bytes 589840 | tf_op jit(solution)/shard_map/reduce_scatter | solution.py:356
  1464.8 57.9 %reduce-scatter.56.cloned.1.call-done = f32[1152,128]{1,0:T(8,128)} async-done(((f32[1152,1024]{1,0:T(8,128)}), f32[1152,128]{1,0:T(8,128)}) %reduce-scatter.56.cloned.1.call-update) | async-done | bytes 589840 | tf_op jit(solution)/shard_map/reduce_scatter | solution.py:357
  1522.8 40.0 %reduce-scatter.44.cloned.1.call-done = f32[128,256]{1,0:T(8,128)} async-done(((f32[1024,256]{1,0:T(8,128)}), f32[128,256]{1,0:T(8,128)}) %reduce-scatter.44.cloned.1.call-update) | async-done | bytes 131088 | tf_op jit(solution)/shard_map/reduce_scatter | solution.py:351
  1562.8 40.1 %reduce-scatter.50.cloned.1.call-done = f32[256,128]{1,0:T(8,128)} async-done(((f32[256,1024]{1,0:T(8,128)}), f32[256,128]{1,0:T(8,128)}) %reduce-scatter.50.cloned.1.call-update) | async-done | bytes 131088 | tf_op jit(solution)/shard_map/reduce_scatter | solution.py:354
  1602.9 38.1 %reduce-scatter.46.cloned.1.call-done = f32[128,128]{1,0:T(8,128)} async-done(((f32[1024,128]{1,0:T(8,128)}), f32[128,128]{1,0:T(8,128)}) %reduce-scatter.46.cloned.1.call-update) | async-done | bytes 65552 | tf_op jit(solution)/shard_map/reduce_scatter | solution.py:352
  1641.0 37.7 %reduce-scatter.48.cloned.1.call-done = f32[128,128]{1,0:T(8,128)} async-done(((f32[1024,128]{1,0:T(8,128)}), f32[128,128]{1,0:T(8,128)}) %reduce-scatter.48.cloned.1.call-update) | async-done | bytes 65552 | tf_op jit(solution)/shard_map/reduce_scatter | solution.py:353
  (461 shorter events, 292.8 us)
Async XLA Ops:
  8.0 178.0 %all-gather.16.cloned.1.call-start = ((), (), s32[]{:S(2)}) async-start(), calls=%async_computation.19 | async-start | bytes 1310720 | tf_op jit(solution)/shard_map/all_gather | solution.py:103
  11.7 15.8 collective-permute-start
  14.8 32.3 %collective-permute-start.2 = (bf16[1,256,1024]{2,1,0:T(8,128)(2,1)S(1)}, bf16[1,256,1024]{2,1,0:T(8,128)(2,1)}, u32[]{:S(2)}, u32[]{:S(2)}) collective-permute-start(bf16[1,256,1024]{2,1,0:T(8,128)(2,1)S(1)} %get-tuple-element.349), channel_id=1, source_target_pairs={{0,1},{1,0},{2,3},{3,2},{4,5},{5,4},{6,7},{7,6},{8,9},{9,8},{10,11... | collective-permute-start | bytes 1572872 | tf_op jit(solution)/shard_map/ppermute | solution.py:23
  29.0 72.4 %collective-permute-start.1 = (bf16[2,256,1024]{2,1,0:T(8,128)(2,1)}, bf16[2,256,1024]{2,1,0:T(8,128)(2,1)}, u32[]{:S(2)}, u32[]{:S(2)}) collective-permute-start(bf16[2,256,1024]{2,1,0:T(8,128)(2,1)} %get-tuple-element.359), channel_id=1, source_target_pairs={{0,2},{1,3},{2,0},{3,1},{4,6},{5,7},{6,4},{7,5},{8,10},{9,11},{10,... | collective-permute-start | bytes 3145736 | tf_op jit(solution)/shard_map/ppermute | solution.py:23
  33.1 151.8 %copy-start.12 = (f32[1024,64]{0,1:T(8,128)}, f32[1024,64]{0,1:T(8,128)S(1)}, u32[]{:S(2)}) copy-start(f32[1024,64]{0,1:T(8,128)S(1)} %pad_maximum_fusion.6) | copy-start | bytes 786436
  49.6 71.6 %collective-permute-start.3 = (bf16[2,256,1024]{2,1,0:T(8,128)(2,1)}, bf16[2,256,1024]{2,1,0:T(8,128)(2,1)}, u32[]{:S(2)}, u32[]{:S(2)}) collective-permute-start(bf16[2,256,1024]{2,1,0:T(8,128)(2,1)} %get-tuple-element.363), channel_id=1, source_target_pairs={{0,2},{1,3},{2,0},{3,1},{4,6},{5,7},{6,4},{7,5},{8,10},{9,11},{10,... | collective-permute-start | bytes 3145736 | tf_op jit(solution)/shard_map/ppermute | solution.py:23
  126.1 59.9 %all-gather.18.cloned.1.call-start = ((), (), s32[]{:S(2)}) async-start(), calls=%async_computation.20 | async-start | bytes 1310720 | tf_op jit(solution)/shard_map/all_gather | solution.py:104
  138.6 138.2 %all-gather.28.cloned.1.call-start = ((), (), s32[]{:S(2)}) async-start(), calls=%async_computation.27 | async-start | bytes 1310720 | tf_op jit(solution)/shard_map/all_gather | solution.py:103
  138.7 137.0 %copy-start.14 = (f32[1024,64]{0,1:T(8,128)}, f32[1024,64]{0,1:T(8,128)S(1)}, u32[]{:S(2)}) copy-start(f32[1024,64]{0,1:T(8,128)S(1)} %pad_maximum_fusion.8) | copy-start | bytes 786436
  141.8 135.0 %all-gather.30.cloned.1.call-start = ((), (), s32[]{:S(2)}) async-start(), calls=%async_computation.28 | async-start | bytes 1310720 | tf_op jit(solution)/shard_map/all_gather | solution.py:104
  171.9 192.8 %reduce-scatter.20.cloned.1.call-start = ((), (), s32[]{:S(2)}) async-start(), calls=%async_computation.21 | async-start | bytes 2621440 | tf_op jit(solution)/shard_map/reduce_scatter | solution.py:253
  275.1 133.1 %reduce-scatter.24.cloned.1.call-start = ((), (), s32[]{:S(2)}) async-start(), calls=%async_computation.29 | async-start | bytes 2621440 | tf_op jit(solution)/shard_map/reduce_scatter | solution.py:253
  364.1 52.6 %all-gather.22.cloned.1.call-start = ((), (), s32[]{:S(2)}) async-start(), calls=%async_computation.23 | async-start | bytes 2654208 | tf_op jit(solution)/shard_map/all_gather | solution.py:87
  364.7 92.9 %all-gather.20.cloned.1.call-start = ((), (), s32[]{:S(2)}) async-start(), calls=%async_computation.22 | async-start | bytes 2621440 | tf_op jit(solution)/shard_map/all_gather | solution.py:261
  409.8 375.8 %copy-start.88 = (f32[256]{0:T(256)}, f32[256]{0:T(256)S(1)}, u32[]{:S(2)}) copy-start(f32[256]{0:T(256)S(1)} %fusion.177) | copy-start | bytes 3076
  409.8 375.8 %copy-start.86 = (f32[256]{0:T(256)}, f32[256]{0:T(256)S(1)}, u32[]{:S(2)}) copy-start(f32[256]{0:T(256)S(1)} %fusion.179) | copy-start | bytes 3076
  412.5 74.4 %all-gather.24.cloned.1.call-start = ((), (), s32[]{:S(2)}) async-start(), calls=%async_computation.24 | async-start | bytes 2654208 | tf_op jit(solution)/shard_map/all_gather | solution.py:88
  413.1 121.0 %all-gather.38.cloned.1.call-start = ((), (), s32[]{:S(2)}) async-start(), calls=%async_computation.49 | async-start | bytes 2621440 | tf_op jit(solution)/shard_map/all_gather | solution.py:285
  414.3 149.7 %all-gather.26.cloned.1.call-start = ((), (), s32[]{:S(2)}) async-start(), calls=%async_computation.25 | async-start | bytes 2654208 | tf_op jit(solution)/shard_map/all_gather | solution.py:89
  415.1 207.8 %all-gather.32.cloned.1.call-start = ((), (), s32[]{:S(2)}) async-start(), calls=%async_computation.30 | async-start | bytes 2621440 | tf_op jit(solution)/shard_map/all_gather | solution.py:261
  415.8 262.9 %all-gather.40.cloned.1.call-start = ((), (), s32[]{:S(2)}) async-start(), calls=%async_computation.50 | async-start | bytes 2621440 | tf_op jit(solution)/shard_map/all_gather | solution.py:285
  416.4 287.9 %reduce-scatter.28.cloned.1.call-start = ((), (), s32[]{:S(2)}) async-start(), calls=%async_computation.32 | async-start | bytes 2621440 | tf_op jit(solution)/shard_map/reduce_scatter | solution.py:294
  582.5 157.7 %reduce-scatter.36.cloned.1.call-start = ((), (), s32[]{:S(2)}) async-start(), calls=%async_computation.37 | async-start | bytes 2621440 | tf_op jit(solution)/shard_map/reduce_scatter | solution.py:294
  697.3 88.4 %reduce-scatter.26.cloned.1.call-start = ((), (), s32[]{:S(2)}) async-start(), calls=%async_computation.31 | async-start | bytes 2621440 | tf_op jit(solution)/shard_map/reduce_scatter | solution.py:267
  704.0 130.3 %all-gather.34.cloned.1.call-start = ((), (), s32[]{:S(2)}) async-start(), calls=%async_computation.33 | async-start | bytes 2621440 | tf_op jit(solution)/shard_map/all_gather | solution.py:304
  789.3 90.8 %all-gather.36.cloned.1.call-start = ((), (), s32[]{:S(2)}) async-start(), calls=%async_computation.38 | async-start | bytes 2621440 | tf_op jit(solution)/shard_map/all_gather | solution.py:304
  790.8 212.3 %reduce-scatter.30.cloned.1.call-start = ((), (), s32[]{:S(2)}) async-start(), calls=%async_computation.34 | async-start | bytes 1310720 | tf_op jit(solution)/shard_map/reduce_scatter | solution.py:319
  874.5 282.6 %reduce-scatter.38.cloned.1.call-start = ((), (), s32[]{:S(2)}) async-start(), calls=%async_computation.39 | async-start | bytes 1310720 | tf_op jit(solution)/shard_map/reduce_scatter | solution.py:319
  923.1 261.4 %reduce-scatter.32.cloned.1.call-start = ((), (), s32[]{:S(2)}) async-start(), calls=%async_computation.35 | async-start | bytes 1310720 | tf_op jit(solution)/shard_map/reduce_scatter | solution.py:322
  924.7 287.2 %reduce-scatter.40.cloned.1.call-start = ((), (), s32[]{:S(2)}) async-start(), calls=%async_computation.40 | async-start | bytes 1310720 | tf_op jit(solution)/shard_map/reduce_scatter | solution.py:322
  930.1 229.1 %copy-start.35 = (f32[1024,2,64]{0,2,1:T(8,128)S(1)}, f32[1024,2,64]{0,2,1:T(8,128)}, u32[]{:S(2)}) copy-start(f32[1024,2,64]{0,2,1:T(8,128)} %copy-done.34) | copy-start | bytes 1572868
  930.1 229.1 %copy-start.37 = (f32[1024,2,64]{0,2,1:T(8,128)S(1)}, f32[1024,2,64]{0,2,1:T(8,128)}, u32[]{:S(2)}) copy-start(f32[1024,2,64]{0,2,1:T(8,128)} %copy-done.36) | copy-start | bytes 1572868
  930.1 229.2 %copy-start.64 = (f32[1024,2]{0,1:T(2,128)S(1)}, f32[1024,2]{0,1:T(2,128)}, u32[]{:S(2)}) copy-start(f32[1024,2]{0,1:T(2,128)} %copy-done.63) | copy-start | bytes 24580
  930.1 229.2 %copy-start.66 = (f32[1024,2]{0,1:T(2,128)S(1)}, f32[1024,2]{0,1:T(2,128)}, u32[]{:S(2)}) copy-start(f32[1024,2]{0,1:T(2,128)} %copy-done.65) | copy-start | bytes 24580
  930.1 229.2 %copy-start.103 = (f32[64]{0:T(128)S(1)}, f32[64]{0:T(128)}, u32[]{:S(2)}) copy-start(f32[64]{0:T(128)} %param.29) | copy-start | bytes 772
  932.9 227.9 %copy-start.79 = (f32[1024,2]{0,1:T(2,128)S(1)}, f32[1024,2]{0,1:T(2,128)}, u32[]{:S(2)}) copy-start(f32[1024,2]{0,1:T(2,128)} %copy-done.78) | copy-start | bytes 24580
  932.9 227.9 %copy-start.81 = (f32[1024,2]{0,1:T(2,128)S(1)}, f32[1024,2]{0,1:T(2,128)}, u32[]{:S(2)}) copy-start(f32[1024,2]{0,1:T(2,128)} %copy-done.80) | copy-start | bytes 24580
  932.9 338.8 %reduce-scatter.34.cloned.1.call-start = ((), (), s32[]{:S(2)}) async-start(), calls=%async_computation.36 | async-start | bytes 2621440 | tf_op jit(solution)/shard_map/reduce_scatter | solution.py:338
  1003.2 156.1 %copy-start.53 = (bf16[1024,2,64]{0,2,1:T(8,128)(2,1)S(1)}, bf16[1024,2,64]{0,2,1:T(8,128)(2,1)}, u32[]{:S(2)}) copy-start(bf16[1024,2,64]{0,2,1:T(8,128)(2,1)} %reduce-scatter.30.cloned.1.call-done) | copy-start | bytes 786436
  1190.2 113.3 %reduce-scatter.42.cloned.1.call-start = ((), (), s32[]{:S(2)}) async-start(), calls=%async_computation.41 | async-start | bytes 2621440 | tf_op jit(solution)/shard_map/reduce_scatter | solution.py:338
  1217.5 131.4 %reduce-scatter.22.cloned.1.call-start = ((), (), s32[]{:S(2)}) async-start(), calls=%async_computation.26 | async-start | bytes 2621440 | tf_op jit(solution)/shard_map/reduce_scatter | solution.py:267
  1224.3 182.4 %reduce-scatter.52.cloned.1.call-start = ((), (), s32[]{:S(2)}) async-start(), calls=%async_computation.46 | async-start | bytes 5308416 | tf_op jit(solution)/shard_map/reduce_scatter | solution.py:355
  1234.2 230.7 %reduce-scatter.54.cloned.1.call-start = ((), (), s32[]{:S(2)}) async-start(), calls=%async_computation.47 | async-start | bytes 5308416 | tf_op jit(solution)/shard_map/reduce_scatter | solution.py:356
  1243.9 278.9 %reduce-scatter.56.cloned.1.call-start = ((), (), s32[]{:S(2)}) async-start(), calls=%async_computation.48 | async-start | bytes 5308416 | tf_op jit(solution)/shard_map/reduce_scatter | solution.py:357
  1254.4 308.4 %reduce-scatter.44.cloned.1.call-start = ((), (), s32[]{:S(2)}) async-start(), calls=%async_computation.42 | async-start | bytes 1179648 | tf_op jit(solution)/shard_map/reduce_scatter | solution.py:351
  1260.5 342.4 %reduce-scatter.50.cloned.1.call-start = ((), (), s32[]{:S(2)}) async-start(), calls=%async_computation.45 | async-start | bytes 1179648 | tf_op jit(solution)/shard_map/reduce_scatter | solution.py:354
  1264.8 376.2 %reduce-scatter.46.cloned.1.call-start = ((), (), s32[]{:S(2)}) async-start(), calls=%async_computation.43 | async-start | bytes 589824 | tf_op jit(solution)/shard_map/reduce_scatter | solution.py:352
  1268.3 410.4 %reduce-scatter.48.cloned.1.call-start = ((), (), s32[]{:S(2)}) async-start(), calls=%async_computation.44 | async-start | bytes 589824 | tf_op jit(solution)/shard_map/reduce_scatter | solution.py:353
  (111 other events, 2084.4 us)
Sparse Core Ops, SparseCore 0:
  126.2 17.8 all-gather.15
  146.2 18.8 all-gather.17
  166.6 16.7 all-gather.27
  184.8 16.7 all-gather.29
  275.2 43.8 reduce-scatter.19
  364.2 43.9 reduce-scatter.23
  582.6 62.7 reduce-scatter.27
  697.4 42.7 reduce-scatter.35
  742.4 43.1 reduce-scatter.25
  874.6 128.5 reduce-scatter.29
  1005.7 151.2 reduce-scatter.37
  1159.6 24.8 reduce-scatter.31
  1187.0 24.8 reduce-scatter.39
  1214.2 43.8 reduce-scatter.33
  1260.2 43.1 reduce-scatter.41
  1305.7 43.1 reduce-scatter.21
  1352.8 53.8 reduce-scatter.51
  1410.9 53.8 reduce-scatter.53
  1468.9 53.8 reduce-scatter.55
  1526.7 36.0 reduce-scatter.43
  1566.9 35.9 reduce-scatter.49
  1606.8 34.0 reduce-scatter.45
  1644.6 34.0 reduce-scatter.47
Sparse Core Ops, SparseCore 1:
  366.4 28.9 all-gather.21
  412.6 44.9 all-gather.19
  459.3 27.6 all-gather.23
  488.5 45.5 all-gather.37
  536.0 28.0 all-gather.25
  565.7 57.1 all-gather.31
  624.4 54.3 all-gather.39
  789.4 44.9 all-gather.33
  835.7 44.3 all-gather.35
